TPU v7x, 128 devices: a whole 4x4x4 slice. The times are simulated.
128 devices in a mesh: src: 8 (over y_lo, x), tgt: 16 (over z, y_hi, core).
Axes of the slice: x: 4, y: 4 (y_hi: 2, y_lo: 2; y = y_hi * 2 + y_lo), z: 4, core: 2. Of those that a mesh axis runs over, the one named last changes fastest.
Arguments:
- residual: bfloat16 [4, 512, 2304], replicated, may hold values from -6 to 6
- targets: bfloat16 [4, 2304, 512], P(None, 'tgt'), may hold values from -6 to 6
- enc_weight: bfloat16 [4, 2304, 16384], P(None, None, ('src', 'tgt')), may hold values from -0.125 to 0.125
- enc_bias: float32 [4, 16384], P(None, ('src', 'tgt')), may hold values from -3 to 3
- active: int32 [4, 512, 16384], P(None, None, ('src', 'tgt')), may hold values 0 or 1
- dec_weight: bfloat16 [80, 2304, 2048], P('src', 'tgt'), may hold values from -0.046875 to 0.046875
- dec_bias: float32 [4, 2304], P(None, 'tgt'), may hold values from -3 to 3
- tile_pairs: int32 [80, 2], P('src'), may hold values from 0 to 3, as said below
Outputs:
- dec_grad: bfloat16 [80, 2304, 2048], P('src', 'tgt')
- enc_grad: bfloat16 [4, 2304, 16384], P(None, None, ('src', 'tgt'))
- bias_grad: float32 [4, 16384], P(None, ('src', 'tgt'))
Inputs may be any that keep to these rules, and one draw needn't show every extreme that they name: `tile_pairs`: rows b * 10 to (b + 1) * 10 - 1 serve latent block b; among them each pair (source, target) with source <= target appears exactly once, source in column 0 and target in column 1.
All inputs are finite; a program needn't handle non-finite values. No bound on the sum of `active` on one device may be relied on, other than what follows from the above.
Results may differ from a plain program's by a relative error of at most 0.019.
Values may be sent and summed in bfloat16 or wider, within the bound.
A program may use at most 128 MiB of HBM per device.

v0:
```python
import jax
import jax.numpy as jnp
from jax import lax
from jax.sharding import PartitionSpec as P


def select_layer(array, index):
    return lax.dynamic_index_in_dim(array, index, 0, keepdims=False)


def add_layer(total, index, value):
    current = lax.dynamic_slice_in_dim(total, index, 1, 0)
    return lax.dynamic_update_slice_in_dim(total, current + value[None], index, 0)


def decoder_term(error_rows, lat_block):
    product = lax.dot_general(
        error_rows, lat_block, (((1,), (0,)), ((), ())), preferred_element_type=jnp.float32
    )
    return product.astype(jnp.bfloat16)


def shards(residual, targets, enc_weight, enc_bias, active, dec_weight, dec_bias, tile_pairs):
    layers = residual.shape[0]
    tok_all = residual.shape[1]
    width_part = targets.shape[1]
    block_width = dec_weight.shape[2]
    mask_own = active.astype(jnp.float32)
    preact = jnp.einsum("lrd,ldc->lrc", residual, enc_weight, preferred_element_type=jnp.float32)
    latent = ((preact + enc_bias[:, None, :]) * mask_own).astype(jnp.bfloat16)
    blocks = lax.all_gather(latent, "tgt", axis=2, tiled=True)
    source_ids = tile_pairs[:, 0]
    target_ids = tile_pairs[:, 1]

    def add_recon(recon_sum, slot_data):
        weight, source, target = slot_data
        lat_block = select_layer(blocks, source)
        recon_term = lax.dot_general(
            weight, lat_block, (((1,), (1,)), ((), ())), preferred_element_type=jnp.float32
        )
        return (add_layer(recon_sum, target, recon_term), None)

    recon_zero = jnp.zeros((layers, width_part, tok_all), jnp.float32)
    recon_sum = lax.scan(add_recon, recon_zero, (dec_weight, source_ids, target_ids))[0]
    whole_sum = lax.psum(recon_sum.astype(jnp.bfloat16), "src").astype(jnp.float32)
    error_part = (whole_sum + dec_bias[:, :, None] - targets.astype(jnp.float32)).astype(
        jnp.bfloat16
    )

    def step_partial(grad_sum, slot_data):
        weight, source, target = slot_data
        error_rows = select_layer(error_part, target)
        lat_block = select_layer(blocks, source)
        lat_term = lax.dot_general(
            error_rows, weight, (((0,), (0,)), ((), ())), preferred_element_type=jnp.float32
        )
        return (add_layer(grad_sum, source, lat_term), decoder_term(error_rows, lat_block))

    grad_zero = jnp.zeros((layers, tok_all, block_width), jnp.float32)
    grad_sum, dec_grad = lax.scan(step_partial, grad_zero, (dec_weight, source_ids, target_ids))
    owned_grad = lax.psum_scatter(
        grad_sum.astype(jnp.bfloat16), "tgt", scatter_dimension=2, tiled=True
    ).astype(jnp.float32)
    pre_grad = (owned_grad * mask_own).astype(jnp.bfloat16)
    enc_grad = jnp.einsum(
        "lrd,lrc->ldc", residual, pre_grad, preferred_element_type=jnp.float32
    ).astype(jnp.bfloat16)
    bias_grad = jnp.sum(pre_grad.astype(jnp.float32), axis=1)
    return (dec_grad, enc_grad, bias_grad)


def solution(mesh):
    in_specs = (
        P(),
        P(None, "tgt", None),
        P(None, None, ("src", "tgt")),
        P(None, ("src", "tgt")),
        P(None, None, ("src", "tgt")),
        P("src", "tgt", None),
        P(None, "tgt"),
        P("src", None),
    )
    out_specs = (P("src", "tgt", None), P(None, None, ("src", "tgt")), P(None, ("src", "tgt")))
    return jax.shard_map(shards, mesh=mesh, in_specs=in_specs, out_specs=out_specs, check_vma=False)
```

profile of v0, /device:TPU:0, one launch (start us, length us, event | category | flops | bytes accessed | tf_op | source)
XLA Modules:
  0.0 544.0 jit_solution(14176928572429023302)
XLA Ops:
  8.8 7.4 %fusion.30 = bf16[4,512,128]{2,1,0:T(8,128)(2,1)} fusion(bf16[4,512,2304]{2,1,0:T(8,128)(2,1)} %param.12, bf16[4,2304,128]{2,1,0:T(8,128)(2,1)S(1)} %copy-done, s32[4,512,128]{2,1,0:T(8,128)} %param.16, f32[4,128]{1,0:T(4,128)} %param.15), kind=kOutput, calls=%fused_computation.28 | convolution fusion | flops 1209008128 | bytes 13371392 | tf_op jit(solution)/shard_map/lrd,ldc->lrc/dot_general | solution.py:29
  16.4 79.1 %all-gather.2.cloned.1.call-done = bf16[4,512,2048]{2,1,0:T(8,128)(2,1)} async-done(((bf16[4,512,128]{2,1,0:T(8,128)(2,1)}), bf16[4,512,2048]{2,1,0:T(8,128)(2,1)}) %all-gather.2.cloned.1.call-update) | async-done | bytes 8388624 | tf_op jit(solution)/shard_map/all_gather | solution.py:31
  95.7 77.2 %while.22 = (s32[]{:T(128)}, f32[4,144,512]{2,1,0:T(8,128)S(1)}, s32[10]{0:T(128)S(1)}, bf16[10,144,2048]{2,1,0:T(8,128)(2,1)}, s32[10]{0:T(128)S(1)}, /*index=5...) while((s32[]{:T(128)}, f32[4,144,512]{2,1,0:T(8,128)S(1)}, s32[10]{0:T(128)S(1)}, ...), condition=%wide.region_1.2_spmd, body=%wide.region_0.1_spmd.sunk | while | flops 302063616 | bytes 3277005 | solution.py:44
  174.0 72.7 %all-reduce.2.cloned.1.call-done = bf16[4,144,512]{2,1,0:T(8,128)(2,1)} async-done(((bf16[4,144,512]{2,1,0:T(8,128)(2,1)}), bf16[4,144,512]{2,1,0:T(8,128)(2,1)}) %all-reduce.2.cloned.1.call-update) | async-done | bytes 589840 | tf_op jit(solution)/shard_map/psum | solution.py:45
  248.1 7.9 %broadcast_in_dim.21 = f32[4,512,2048]{2,1,0:T(8,128)} broadcast(f32[]{:T(128)} %constant.31.clone.1), dimensions={} | broadcast | bytes 16777220 | tf_op jit(solution)/shard_map/broadcast_in_dim | solution.py:59
  255.9 130.4 %while.23 = (s32[]{:T(128)}, f32[4,512,2048]{2,1,0:T(8,128)}, bf16[10,144,2048]{2,1,0:T(8,128)(2,1)}, s32[10]{0:T(128)S(1)}, s32[10]{0:T(128)S(1)}, /*index=5*/b...) while((s32[]{:T(128)}, f32[4,512,2048]{2,1,0:T(8,128)}, ...), condition=%wide.region_4.5_spmd, body=%wide.region_3.4_spmd.sunk | while | flops 605323264 | bytes 11960553 | solution.py:60
  263.9 5.1 fusion.50
  274.0 2.9 fusion.51
  276.9 5.1 fusion.50
  290.0 5.1 fusion.50
  303.0 5.1 fusion.50
  316.0 5.1 fusion.50
  329.0 5.1 fusion.50
  342.1 5.1 fusion.50
  355.1 5.1 fusion.50
  365.3 2.9 fusion.51
  368.2 5.1 fusion.50
  381.3 5.1 fusion.50
  386.3 9.1 %convert_element_type.45 = bf16[4,512,2048]{2,1,0:T(8,128)(2,1)} convert(f32[4,512,2048]{2,1,0:T(8,128)} %get-tuple-element.80) | non-fusion elementwise | flops 4194304 | bytes 25165824 | tf_op jit(solution)/shard_map/convert_element_type | solution.py:62
  395.4 14.6 %copy.16 = bf16[4,512,2048]{1,0,2:T(4,128)(2,1)} copy(bf16[4,512,2048]{2,1,0:T(8,128)(2,1)} %convert_element_type.45) | data formatting | bytes 16777216
  410.0 10.2 %copy.18 = bf16[256,8,4,512]{3,1,2,0:T(8,128)(2,1)} copy(bf16[256,8,4,512]{3,2,1,0:T(4,128)(2,1)} %bitcast.81) | data formatting | bytes 16777216
  420.3 102.1 %reduce-scatter.4.cloned.1.call-done = bf16[128,2048]{1,0:T(8,128)(2,1)} async-done(((bf16[2048,2048]{1,0:T(8,128)(2,1)}), bf16[128,2048]{1,0:T(8,128)(2,1)}) %reduce-scatter.4.cloned.1.call-update) | async-done | bytes 524304
  526.3 6.9 %fusion.28 = bf16[4,2304,128]{1,2,0:T(8,128)(2,1)} fusion(bf16[4,512,2304]{2,1,0:T(8,128)(2,1)} %param.12, bf16[4,512,128]{2,1,0:T(8,128)(2,1)S(1)} %copy.17, s32[4,512,128]{2,1,0:T(8,128)} %param.16), kind=kOutput, calls=%fused_computation.25 | convolution fusion | flops 1210187776 | bytes 13369344 | tf_op jit(solution)/shard_map/lrd,lrc->ldc/dot_general | solution.py:65
  533.2 4.3 copy.14
  (82 shorter events, 81.3 us)
Async XLA Ops:
  7.2 1.7 copy-start
  7.2 9.2 %copy-start.4 = (s32[10,2]{0,1:T(2,128)S(1)}, s32[10,2]{0,1:T(2,128)}, u32[]{:S(2)}) copy-start(s32[10,2]{0,1:T(2,128)} %param.19) | copy-start | bytes 244
  7.2 88.3 %all-gather.2.cloned.1.call-start = ((), (), s32[]{:S(2)}) async-start(), calls=%async_computation.1 | async-start | bytes 8912896 | tf_op jit(solution)/shard_map/all_gather | solution.py:31
  16.3 230.4 %all-reduce.2.cloned.1.call-start = ((), (), s32[]{:S(2)}) async-start(), calls=%async_computation.2 | async-start | bytes 1179648 | tf_op jit(solution)/shard_map/psum | solution.py:45
  95.7 151.1 %copy-start.2 = (bf16[4,144,512]{2,1,0:T(8,128)(2,1)S(1)}, bf16[4,144,512]{2,1,0:T(8,128)(2,1)}, u32[]{:S(2)}) copy-start(bf16[4,144,512]{2,1,0:T(8,128)(2,1)} %param.13) | copy-start | bytes 1769476
  95.7 151.1 %copy-start.3 = (f32[4,144]{1,0:T(4,128)S(1)}, f32[4,144]{1,0:T(4,128)}, u32[]{:S(2)}) copy-start(f32[4,144]{1,0:T(4,128)} %param.18) | copy-start | bytes 6916
  173.8 348.6 %reduce-scatter.4.cloned.1.call-start = ((), (), s32[]{:S(2)}) async-start(), calls=%async_computation.3 | async-start | bytes 8912896
  524.2 13.3 %copy-start.1 = (bf16[4,2304,128]{2,1,0:T(8,128)(2,1)S(1)}, bf16[4,2304,128]{2,1,0:T(8,128)(2,1)}, u32[]{:S(2)}) copy-start(bf16[4,2304,128]{2,1,0:T(8,128)(2,1)} %param.14) | copy-start | bytes 7077892
Sparse Core Ops, SparseCore 0:
  16.4 79.0 all-gather.1
  173.9 72.7 all-reduce.1
  420.4 101.9 reduce-scatter.3
where the time goes:
time: 547 us; the launch traced here: 544 us
  waiting for transfers between devices  254 us (46%)
  matrix products  121 us (22%)
  loops' own time  78 us (14%)
  local copies, waits for them, and re-layouts  64 us (12%)
  between operations  13.8 us (3%)
  other arithmetic  13.4 us (2%)
    unnamed x4, waiting for transfers between devices  102 us
    all_gather x1, waiting for transfers between devices, shards(): blocks = lax.all_gather(latent, 'tgt', axis=2, tiled=True)  79.1 us
    psum x1, waiting for transfers between devices, shards(): lax.psum(recon_sum.astype(jnp.bfloat16), 'src').astype(jnp.float32)  72.7 us
    dot_general x10, matrix products, step_partial(): lax.dot_general(error_rows, weight, (((0,), (0,)), ((), ())), preferred_e...  50.8 us
    another operation x1, loops' own time, shards(): lax.scan(add_recon, recon_zero, (dec_weight, source_ids, target_ids))[0]  39.1 us
    another operation x1, loops' own time, shards(): lax.scan(step_partial, grad_zero, (dec_weight, source_ids, target_ids))  38.9 us
    unnamed x15, local copies, waits for them, and re-layouts  32.6 us
    dot_general x10, matrix products, decoder_term(): lax.dot_general(error_rows, lat_block, (((1,), (0,)), ((), ())), preferre...  29 us
  transfers between devices with their start and end apart: 3, of which 3 were waited for; matrix products, arithmetic and copies ran while one was open for 0% of the time, Pallas kernels for 0%

commit v1 on v0

v1 whole, which is shorter than its diff:
```python
import functools

import jax
import jax.numpy as jnp
from jax import lax
from jax.experimental import pallas as pl
from jax.experimental.pallas import tpu as pltpu
from jax.sharding import PartitionSpec as P

MESH = pl.DeviceIdType.MESH
F32 = jnp.float32
BF16 = jnp.bfloat16
LAYERS = 4
HALVES = 2
ITEMS = LAYERS * HALVES
A_Y, A_OWN_UP, A_OWN_DOWN, A_PAIR_UP, A_PAIR_DOWN, A_FWD_UP, A_FWD_DOWN, A_TWIN = range(8)
R_TWIN, R_RELAY_UP, R_RELAY_DOWN, R_LAST_UP, R_LAST_DOWN, R_Y = range(6)


def column_of(row, size):
    down = lax.broadcasted_iota(jnp.int32, (size, size), 0)
    across = lax.broadcasted_iota(jnp.int32, (size, size), 1)
    spread = jnp.where(down == across, jnp.broadcast_to(row, (size, size)), 0.0)
    return jnp.sum(spread, axis=1, keepdims=True)


def kernel(
    res_hbm, tgt_hbm, encw_hbm, encb_ref, act_hbm, decw_hbm, decb_ref, pairs_ref,
    dec_hbm, enc_hbm, bias_ref,
    res_v, tgt_v, encw_v, act_v, w_v, lat_v, p_acc, p_snd, p_rcv, err_v, g_v, tw_v, s_v,
    zr_v, zf_v, ty_v, yr_v, pre_v, dst_v, eo_v, row_s,
    res_sem, encw_sem, act_sem, w_sem, tgt_sem, dst_sem, eo_sem,
    a_send, a_recv, r_send, r_recv, p_send, p_recv, e_send, e_recv,
):
    tok = res_v.shape[1]
    chunk = tok // HALVES
    part = chunk // 2
    feats = w_v.shape[1]
    width = res_v.shape[2]

    src = lax.axis_index("src")
    tgt = lax.axis_index("tgt")
    x, yl = lax.rem(src, 4), src // 4
    z, yh, core = tgt // 4, lax.rem(tgt // 2, 2), lax.rem(tgt, 2)
    up, down, far = lax.rem(z + 1, 4), lax.rem(z + 3, 4), lax.rem(z + 2, 4)
    place = z * 2 + yh

    def device(zz, hh, cc):
        return (src, zz * 4 + hh * 2 + cc)

    dev_up, dev_down = device(up, yh, core), device(down, yh, core)
    dev_y, dev_twin = device(z, 1 - yh, core), device(z, yh, 1 - core)
    peers = [lax.rem(src + d, 8) for d in range(8)]

    def at128(value):
        return pl.multiple_of(value, 128)

    def half_of(cc):
        return pl.ds(at128(cc * 1024), 1024)

    def block_of(q):
        return pl.ds(at128(core * 1024 + q * 128), 128)

    def pair_of(zz):
        return pl.ds(at128(core * 1024 + zz * 256), 256)

    def pair(zz):
        return pl.ds(at128(zz * 256), 256)

    incoming = {}

    def fetch(name, source, target, sem):
        copy = pltpu.make_async_copy(source, target, sem)
        copy.start()
        incoming[name] = copy

    for s in range(LAYERS):
        fetch(("encw", s), encw_hbm.at[s], encw_v.at[s], encw_sem.at[s])
        fetch(("res", s), res_hbm.at[s], res_v.at[s], res_sem.at[s])
        fetch(("act", s), act_hbm.at[s], act_v.at[s], act_sem.at[s])
    for j in range(16):
        cc, q = j % 2, j // 2
        fetch(
            ("w", j),
            decw_hbm.at[:, :, pl.ds(j * 128, 128)],
            w_v.at[:, :, pl.ds(cc * 1024 + q * 128, 128)],
            w_sem.at[j],
        )
    fetch("tgt", tgt_hbm.at[x], tgt_v, tgt_sem)

    for s in range(LAYERS):
        for t in range(s, LAYERS):
            found = jnp.int32(0)
            for k in range(10):
                hit = jnp.logical_and(pairs_ref[k, 0] == s, pairs_ref[k, 1] == t)
                found = jnp.where(hit, jnp.int32(k), found)
            row_s[s * 4 + t] = found

    barrier = pltpu.get_barrier_semaphore()
    greeted = [dev_up, dev_down, dev_y, dev_twin] + [(peers[d], tgt) for d in range(1, 8)]
    for other in greeted:
        pl.semaphore_signal(barrier, inc=1, device_id=other, device_id_type=MESH)
    pl.semaphore_wait(barrier, len(greeted))

    sent = []

    def remote(source, target, send_sem, recv_sem, dev):
        return pltpu.make_async_remote_copy(
            src_ref=source, dst_ref=target, send_sem=send_sem, recv_sem=recv_sem,
            device_id=dev, device_id_type=MESH,
        )

    def gather_copy(i, kind):
        lat = lat_v.at[i]
        if kind in (A_Y, A_OWN_UP, A_OWN_DOWN):
            view = lat.at[:, block_of(place)]
        elif kind in (A_PAIR_UP, A_PAIR_DOWN):
            view = lat.at[:, block_of(z * 2 + 1 - yh)]
        elif kind == A_FWD_UP:
            view = lat.at[pl.ds(0, part), pair_of(down)]
        elif kind == A_FWD_DOWN:
            view = lat.at[pl.ds(part, part), pair_of(up)]
        else:
            view = lat.at[:, half_of(core)]
        if kind == A_Y:
            dev = dev_y
        elif kind == A_TWIN:
            dev = dev_twin
        elif kind in (A_OWN_UP, A_PAIR_UP, A_FWD_UP):
            dev = dev_up
        else:
            dev = dev_down
        return remote(view, view, a_send.at[i, kind], a_recv.at[i, kind], dev)

    def scatter_copy(i, kind):
        if kind == R_TWIN:
            source, target, dev = g_v.at[i, :, half_of(1 - core)], tw_v.at[i], dev_twin
        elif kind == R_RELAY_UP:
            source, target, dev = s_v.at[i, pl.ds(0, part), pair(far)], zr_v.at[i, 0], dev_up
        elif kind == R_RELAY_DOWN:
            source, target, dev = s_v.at[i, pl.ds(part, part), pair(far)], zr_v.at[i, 1], dev_down
        elif kind == R_LAST_UP:
            source, target, dev = s_v.at[i, :, pair(up)], zf_v.at[i, 0], dev_up
        elif kind == R_LAST_DOWN:
            source, target, dev = s_v.at[i, :, pair(down)], zf_v.at[i, 1], dev_down
        else:
            source, target, dev = ty_v.at[i], yr_v.at[i], dev_y
        return remote(source, target, r_send.at[i, kind], r_recv.at[i, kind], dev)

    def part_copy(h, d):
        peer = peers[d]
        source = p_snd.at[h, lax.rem(peer, 4), :, pl.ds(at128((peer // 4) * 128), 128)]
        return remote(source, p_rcv.at[h, d], p_send.at[h, d], p_recv.at[h, d], (peer, tgt))

    def error_copy(h, d):
        view = err_v.at[h, x, :, pl.ds(at128(yl * 128), 128)]
        return remote(view, view, e_send.at[h, d], e_recv.at[h, d], (peers[d], tgt))

    def start(copy):
        copy.start()
        sent.append(copy)

    def encode(h, s):
        i = h * 4 + s
        if h == 0:
            for name in ("encw", "res", "act"):
                incoming[(name, s)].wait()
        rows = pl.ds(h * chunk, chunk)
        pre = jnp.dot(res_v[s, rows, :], encw_v[s], preferred_element_type=F32)
        pre = pre + encb_ref[s : s + 1, :]
        lat_v[i, :, block_of(place)] = (pre * act_v[s, rows, :].astype(F32)).astype(BF16)
        for kind in (A_Y, A_OWN_UP, A_OWN_DOWN):
            start(gather_copy(i, kind))

    def gather_pair(i):
        gather_copy(i, A_Y).wait_recv()
        start(gather_copy(i, A_PAIR_UP))
        start(gather_copy(i, A_PAIR_DOWN))

    def gather_forward(i):
        gather_copy(i, A_OWN_UP).wait_recv()
        gather_copy(i, A_PAIR_UP).wait_recv()
        start(gather_copy(i, A_FWD_UP))
        gather_copy(i, A_OWN_DOWN).wait_recv()
        gather_copy(i, A_PAIR_DOWN).wait_recv()
        start(gather_copy(i, A_FWD_DOWN))

    def gather_twin(i):
        gather_copy(i, A_FWD_UP).wait_recv()
        gather_copy(i, A_FWD_DOWN).wait_recv()
        start(gather_copy(i, A_TWIN))

    def recon(h, s):
        i = h * 4 + s
        gather_copy(i, A_TWIN).wait_recv()
        if i == 0:
            for j in range(16):
                incoming[("w", j)].wait()
        for t in range(s, LAYERS):
            term = lax.dot_general(
                w_v[row_s[s * 4 + t]], lat_v[i], (((1,), (1,)), ((), ())),
                preferred_element_type=F32,
            )
            if s == 0:
                p_acc[h, t] = term
            else:
                p_acc[h, t] = p_acc[h, t] + term

    def share_parts(h):
        p_snd[h] = p_acc[h].astype(BF16)
        for d in range(1, 8):
            start(part_copy(h, d))

    def make_error(h):
        own = pl.ds(at128(yl * 128), 128)
        total = p_acc[h, x, :, own]
        for d in range(1, 8):
            part_copy(h, d).wait_recv()
            total = total + p_rcv[h, d].astype(F32)
        if h == 0:
            incoming["tgt"].wait()
        bias = column_of(decb_ref[pl.ds(x, 1), :], feats)
        wanted = tgt_v[:, pl.ds(at128(h * chunk + yl * 128), 128)].astype(F32)
        err_v[h, x, :, own] = (total + bias - wanted).astype(BF16)
        for d in range(1, 8):
            start(error_copy(h, d))

    def have_error(h):
        for d in range(1, 8):
            error_copy(h, d).wait_recv()

    def grad(h, s):
        i = h * 4 + s
        count = LAYERS - s
        err = err_v[h, s:].reshape(count * feats, chunk)
        step = 512

        @pl.loop(0, 2048 // step)
        def _(n):
            cols = pl.ds(pl.multiple_of(n * step, step), step)
            weights = [w_v[row_s[s * 4 + t], :, cols] for t in range(s, LAYERS)]
            stack = jnp.concatenate(weights, axis=0) if count > 1 else weights[0]
            g_v[i, :, cols] = lax.dot_general(
                err, stack, (((0,), (0,)), ((), ())), preferred_element_type=F32
            ).astype(BF16)

        start(scatter_copy(i, R_TWIN))

    def scatter_twin(i):
        scatter_copy(i, R_TWIN).wait_recv()
        s_v[i] = (g_v[i, :, half_of(core)].astype(F32) + tw_v[i].astype(F32)).astype(BF16)
        start(scatter_copy(i, R_RELAY_UP))
        start(scatter_copy(i, R_RELAY_DOWN))

    def scatter_relay(i):
        for kind, rows, to, slot, last in (
            (R_RELAY_UP, pl.ds(0, part), up, 0, R_LAST_UP),
            (R_RELAY_DOWN, pl.ds(part, part), down, 1, R_LAST_DOWN),
        ):
            scatter_copy(i, kind).wait_recv()
            mine = s_v[i, rows, pair(to)].astype(F32)
            s_v[i, rows, pair(to)] = (mine + zr_v[i, slot].astype(F32)).astype(BF16)
            start(scatter_copy(i, last))

    def column_sum(i, hh):
        inner = pl.ds(at128(hh * 128), 128)
        mine = s_v[i, :, pl.ds(at128(z * 256 + hh * 128), 128)].astype(F32)
        return mine + zf_v[i, 0, :, inner].astype(F32) + zf_v[i, 1, :, inner].astype(F32)

    def scatter_last(i):
        scatter_copy(i, R_LAST_UP).wait_recv()
        scatter_copy(i, R_LAST_DOWN).wait_recv()
        ty_v[i] = column_sum(i, 1 - yh).astype(BF16)
        start(scatter_copy(i, R_Y))

    def scatter_own(h, s):
        i = h * 4 + s
        scatter_copy(i, R_Y).wait_recv()
        rows = pl.ds(h * chunk, chunk)
        grads = column_sum(i, yh) + yr_v[i].astype(F32)
        pre = (grads * act_v[s, rows, :].astype(F32)).astype(BF16)
        pre_v[s, rows, :] = pre
        sums = jnp.sum(pre.astype(F32), axis=0, keepdims=True)
        if h == 0:
            bias_ref[s : s + 1, :] = sums
        else:
            bias_ref[s : s + 1, :] = bias_ref[s : s + 1, :] + sums

    leaving = {}

    def encoder_grad(s, slot):
        if ("enc", slot) in leaving:
            leaving.pop(("enc", slot)).wait()

        @pl.loop(0, width // 256)
        def _(n):
            cols = pl.ds(pl.multiple_of(n * 256, 256), 256)
            eo_v[slot, cols, :] = lax.dot_general(
                res_v[s, :, cols], pre_v[s], (((0,), (0,)), ((), ())), preferred_element_type=F32
            ).astype(BF16)

        copy = pltpu.make_async_copy(eo_v.at[slot], enc_hbm.at[s], eo_sem.at[slot])
        copy.start()
        leaving[("enc", slot)] = copy

    def decoder_grad(k):
        slot = k % 2
        if ("dec", slot) in leaving:
            leaving.pop(("dec", slot)).wait()
        source, target = pairs_ref[k, 0], pairs_ref[k, 1]
        low, high = err_v[0, target], err_v[1, target]
        for cc in range(2):
            for m in range(2):
                cols = slice(cc * 1024 + m * 512, cc * 1024 + (m + 1) * 512)
                out = jnp.dot(low, lat_v[source, :, cols], preferred_element_type=F32)
                out = out + jnp.dot(high, lat_v[source + 4, :, cols], preferred_element_type=F32)
                out = out.astype(BF16)
                for j in range(4):
                    begin = ((m * 4 + j) * 2 + cc) * 128
                    dst_v[slot, :, begin : begin + 128] = out[:, j * 128 : (j + 1) * 128]
        copy = pltpu.make_async_copy(dst_v.at[slot], dec_hbm.at[k], dst_sem.at[slot])
        copy.start()
        leaving[("dec", slot)] = copy

    for h in range(HALVES):
        for s in range(LAYERS):
            encode(h, s)
    for step in range(ITEMS + 3):
        if step < ITEMS:
            gather_pair(step)
        if 0 <= step - 1 < ITEMS:
            gather_forward(step - 1)
        if 0 <= step - 2 < ITEMS:
            gather_twin(step - 2)
        if step - 3 >= 0:
            recon((step - 3) // 4, (step - 3) % 4)
        if step == 6:
            share_parts(0)
        if step == 8:
            make_error(0)
    share_parts(1)
    have_error(0)
    order = [(h, s) for h in range(HALVES) for s in reversed(range(LAYERS))]
    index = [h * 4 + s for h, s in order]
    rows_done = 0
    for step in range(ITEMS + 4):
        if step == 4:
            have_error(1)
        if step < ITEMS:
            grad(*order[step])
        if step == 1:
            make_error(1)
        if 0 <= step - 1 < ITEMS:
            scatter_twin(index[step - 1])
        if 0 <= step - 2 < ITEMS:
            scatter_relay(index[step - 2])
        if 0 <= step - 3 < ITEMS:
            scatter_last(index[step - 3])
        if step - 4 >= 0:
            h, s = order[step - 4]
            scatter_own(h, s)
            if h == 1:
                encoder_grad(s, s % 2)
        if step >= 4:
            for _ in range(2):
                if rows_done < 10:
                    decoder_grad(rows_done)
                    rows_done += 1
    for copy in leaving.values():
        copy.wait()
    for copy in sent:
        copy.wait_send()


def shards(residual, targets, enc_weight, enc_bias, active, dec_weight, dec_bias, tile_pairs):
    layers, tok, width = residual.shape
    feats = targets.shape[1]
    own = enc_weight.shape[2]
    rows, _, block = dec_weight.shape
    chunk = tok // HALVES
    any_space = pl.BlockSpec(memory_space=pl.ANY)
    vmem = pl.BlockSpec(memory_space=pltpu.VMEM)
    dma = pltpu.SemaphoreType.DMA
    return pl.pallas_call(
        kernel,
        out_shape=(
            jax.ShapeDtypeStruct((rows, feats, block), BF16),
            jax.ShapeDtypeStruct((layers, width, own), BF16),
            jax.ShapeDtypeStruct((layers, own), F32),
        ),
        in_specs=[
            any_space, any_space, any_space, vmem, any_space, any_space, vmem,
            pl.BlockSpec(memory_space=pltpu.SMEM),
        ],
        out_specs=(any_space, any_space, vmem),
        scratch_shapes=[
            pltpu.VMEM((layers, tok, width), BF16),
            pltpu.VMEM((feats, tok), BF16),
            pltpu.VMEM((layers, width, own), BF16),
            pltpu.VMEM((layers, tok, own), jnp.int32),
            pltpu.VMEM((rows, feats, block), BF16),
            pltpu.VMEM((ITEMS, chunk, block), BF16),
            pltpu.VMEM((HALVES, layers, feats, chunk), F32),
            pltpu.VMEM((HALVES, layers, feats, chunk), BF16),
            pltpu.VMEM((HALVES, 8, feats, 128), BF16),
            pltpu.VMEM((HALVES, layers, feats, chunk), BF16),
            pltpu.VMEM((ITEMS, chunk, block), BF16),
            pltpu.VMEM((ITEMS, chunk, block // 2), BF16),
            pltpu.VMEM((ITEMS, chunk, block // 2), BF16),
            pltpu.VMEM((ITEMS, 2, chunk // 2, 256), BF16),
            pltpu.VMEM((ITEMS, 2, chunk, 256), BF16),
            pltpu.VMEM((ITEMS, chunk, own), BF16),
            pltpu.VMEM((ITEMS, chunk, own), BF16),
            pltpu.VMEM((layers, tok, own), BF16),
            pltpu.VMEM((2, feats, block), BF16),
            pltpu.VMEM((2, width, own), BF16),
            pltpu.SMEM((16,), jnp.int32),
            dma((layers,)), dma((layers,)), dma((layers,)), dma((16,)), dma, dma((2,)), dma((2,)),
            dma((ITEMS, 8)), dma((ITEMS, 8)), dma((ITEMS, 6)), dma((ITEMS, 6)),
            dma((HALVES, 8)), dma((HALVES, 8)), dma((HALVES, 8)), dma((HALVES, 8)),
        ],
        compiler_params=pltpu.CompilerParams(
            collective_id=0, has_side_effects=True, vmem_limit_bytes=67043328
        ),
    )(residual, targets, enc_weight, enc_bias, active, dec_weight, dec_bias, tile_pairs)


def solution(mesh):
    in_specs = (
        P(),
        P(None, "tgt", None),
        P(None, None, ("src", "tgt")),
        P(None, ("src", "tgt")),
        P(None, None, ("src", "tgt")),
        P("src", "tgt", None),
        P(None, "tgt"),
        P("src", None),
    )
    out_specs = (P("src", "tgt", None), P(None, None, ("src", "tgt")), P(None, ("src", "tgt")))
    return jax.shard_map(shards, mesh=mesh, in_specs=in_specs, out_specs=out_specs, check_vma=False)
```

time: 547 us -> 120 us (0.22)
  waiting for transfers between devices: 254 us -> 0 us
  matrix products: 121 us -> 0 us
  Pallas kernels: 0 us -> 109 us
  loops' own time: 78 us -> 0 us
  local copies, waits for them, and re-layouts: 64 us -> 9.77 us
  other arithmetic: 13.4 us -> 0 us
  between operations: 13.8 us -> 0.66 us
    dot_general x32 -> x0, matrix products: 121 us -> none  [the longest x10 50.8 us: step_partial(): lax.dot_general(error_rows, weight, (((0,), (0,)), ((), ())), preferred_e...]
    pallas_call x0 -> x1, Pallas kernels: none -> 109 us  [shards(): pl.pallas_call(kernel, out_shape=(jax.ShapeDtypeStruct((rows, feats, bloc...]
    unnamed x4 -> x0, waiting for transfers between devices: 102 us -> none
    all_gather x1 -> x0, waiting for transfers between devices: 79.1 us -> none  [shards(): blocks = lax.all_gather(latent, 'tgt', axis=2, tiled=True)]
    another operation x2 -> x0, loops' own time: 78 us -> none  [the longest x1 39.1 us: shards(): lax.scan(add_recon, recon_zero, (dec_weight, source_ids, target_ids))[0]]
    psum x1 -> x0, waiting for transfers between devices: 72.7 us -> none  [shards(): lax.psum(recon_sum.astype(jnp.bfloat16), 'src').astype(jnp.float32)]
    dynamic_slice x40 -> x0, local copies, waits for them, and re-layouts: 23.5 us -> none  [shards(): lax.scan(add_recon, recon_zero, (dec_weight, source_ids, target_ids))[0]]
    unnamed x15 -> x8, local copies, waits for them, and re-layouts: 32.6 us -> 9.77 us
  transfers between devices with their start and end apart: 3 -> 0, of which waited for: 3 -> 0; matrix products, arithmetic and copies ran while one was open for 0% -> 0% of each run, Pallas kernels for 0% -> 0%
where the time goes in v1:
time: 120 us
  Pallas kernels  109 us (91%)
  local copies, waits for them, and re-layouts  9.77 us (8%)
    pallas_call x1, Pallas kernels, shards(): pl.pallas_call(kernel, out_shape=(jax.ShapeDtypeStruct((rows, feats, bloc...  109 us
    unnamed x8, local copies, waits for them, and re-layouts  9.77 us

profile of v1, /device:TPU:0, one launch (start us, length us, event | category | flops | bytes accessed | tf_op | source)
XLA Modules:
  0.0 119.6 jit_solution(3400648903309432368)
XLA Ops:
  0.6 1.4 %copy.11.pairs_ref = s32[10,2]{1,0:T(8,128)} copy(s32[10,2]{0,1:T(2,128)} %param.15) | data formatting | bytes 160 | tf_op args[7]
  2.0 109.2 %shard_map.103 = (bf16[10,144,2048]{2,1,0:T(8,128)(2,1)}, bf16[4,2304,128]{2,1,0:T(8,128)(2,1)}, f32[4,128]{1,0:T(4,128)}) custom-call(bf16[4,512,2304]{2,1,0:T(8,128)(2,1)} %res_hbm.1, bf16[4,144,512]{2,1,0:T(8,128)(2,1)} %tgt_hbm.1, bf16[4,2304,128]{2,1,0:T(8,128)(2,1)} %encw_hbm.1, f32[4,128]{1,0:T(4,128)} %encb_ref.1, s32[4,512,128]{2,1,0:T(8,128)} %act_hbm.1, ...), custom_call_target="tpu_custom_call" | custom-call | tf_op jit(solution)/shard_map/pallas_call | solution.py:384
  111.2 0.0 copy-start
  111.2 0.0 copy-start.1
  111.2 6.4 %copy.15 = bf16[10,144,2048]{2,1,0:T(8,128)(2,1)} copy(bf16[10,144,2048]{2,1,0:T(8,128)(2,1)} %get-tuple-element.6) | data formatting | bytes 11796480
  117.6 0.0 copy-done
  117.7 1.4 %copy.16 = bf16[4,2304,128]{2,1,0:T(8,128)(2,1)} copy(bf16[4,2304,128]{2,1,0:T(8,128)(2,1)S(1)} %copy-done) | data formatting | bytes 4718592
  119.1 0.0 copy-done.1
  119.1 0.6 copy.17
Async XLA Ops:
  111.2 6.4 %copy-start = (bf16[4,2304,128]{2,1,0:T(8,128)(2,1)S(1)}, bf16[4,2304,128]{2,1,0:T(8,128)(2,1)}, u32[]{:S(2)}) copy-start(bf16[4,2304,128]{2,1,0:T(8,128)(2,1)} %get-tuple-element.7) | copy-start | bytes 7077892
  111.2 7.8 %copy-start.1 = (f32[4,128]{1,0:T(4,128)S(1)}, f32[4,128]{1,0:T(4,128)}, u32[]{:S(2)}) copy-start(f32[4,128]{1,0:T(4,128)} %get-tuple-element.8) | copy-start | bytes 6148

commit v2 on v1

v2 whole, which is shorter than its diff:
```python
import functools

import jax
import jax.numpy as jnp
from jax import lax
from jax.experimental import pallas as pl
from jax.experimental.pallas import tpu as pltpu
from jax.sharding import PartitionSpec as P

MESH = pl.DeviceIdType.MESH
F32 = jnp.float32
BF16 = jnp.bfloat16
LAYERS = 4
HALVES = 2
ITEMS = LAYERS * HALVES
A_Y, A_OWN_UP, A_OWN_DOWN, A_PAIR_UP, A_PAIR_DOWN, A_FWD_UP, A_FWD_DOWN, A_FAR, A_TWIN = range(9)
R_TWIN, R_FAR, R_SIDE_UP, R_SIDE_DOWN, R_RELAY_UP, R_RELAY_DOWN, R_OWN_UP, R_OWN_DOWN, R_Y = range(9)


def column_of(row, size):
    down = lax.broadcasted_iota(jnp.int32, (size, size), 0)
    across = lax.broadcasted_iota(jnp.int32, (size, size), 1)
    spread = jnp.where(down == across, jnp.broadcast_to(row, (size, size)), 0.0)
    return jnp.sum(spread, axis=1, keepdims=True)


def kernel(
    res_hbm, tgt_hbm, encw_hbm, encb_ref, act_hbm, decw_hbm, decb_ref, pairs_ref,
    dec_ref, enc_ref, bias_ref,
    res_v, tgt_v, encw_v, act_v, w_v, lat_v, p_acc, p_snd, p_rcv, err_v, g_v, tw_v, s_v,
    fy_v, zr_v, zf_v, ty_v, yr_v, pre_v, et_v, row_s,
    res_sem, encw_sem, act_sem, w_sem, tgt_sem,
    a_send, a_recv, r_send, r_recv, p_send, p_recv, e_send, e_recv,
):
    tok = tgt_v.shape[1]
    chunk = tok // HALVES
    part = chunk // 2
    feats = w_v.shape[1]
    blocks = res_v.shape[1]

    src = lax.axis_index("src")
    tgt = lax.axis_index("tgt")
    x, yl = lax.rem(src, 4), src // 4
    z, yh, core = tgt // 4, lax.rem(tgt // 2, 2), lax.rem(tgt, 2)
    up, down, far = lax.rem(z + 1, 4), lax.rem(z + 3, 4), lax.rem(z + 2, 4)
    place = z * 2 + yh

    def device(zz, hh, cc):
        return (src, zz * 4 + hh * 2 + cc)

    dev_up, dev_down = device(up, yh, core), device(down, yh, core)
    dev_y, dev_twin = device(z, 1 - yh, core), device(z, yh, 1 - core)
    peers = [lax.rem(src + d, 8) for d in range(8)]

    def at128(value):
        return pl.multiple_of(value, 128)

    def half_of(cc):
        return pl.ds(at128(cc * 1024), 1024)

    def block_of(q):
        return pl.ds(at128(core * 1024 + q * 128), 128)

    barrier = pltpu.get_barrier_semaphore()
    greeted = [dev_up, dev_down, dev_y, dev_twin] + [(peers[d], tgt) for d in range(1, 8)]
    for other in greeted:
        pl.semaphore_signal(barrier, inc=1, device_id=other, device_id_type=MESH)

    incoming = {}

    def fetch(name, source, target, sem):
        copy = pltpu.make_async_copy(source, target, sem)
        copy.start()
        incoming[name] = copy

    def fetch_layer(s):
        fetch(("encw", s), encw_hbm.at[s], encw_v.at[s], encw_sem.at[s])
        fetch_tokens(0, s)
        fetch(("act", s), act_hbm.at[s], act_v.at[s], act_sem.at[s])

    def fetch_tokens(h, s):
        for n in range(blocks):
            pltpu.make_async_copy(
                res_hbm.at[s, pl.ds(h * chunk, chunk), pl.ds(n * 256, 256)],
                res_v.at[s, n, h],
                res_sem.at[s, h],
            ).start()

    def have_tokens(h, s):
        whole = res_v.at[s, :, h]
        pltpu.make_async_copy(whole, whole, res_sem.at[s, h]).wait()

    def fetch_rest():
        for j in range(16):
            cc, q = j % 2, j // 2
            fetch(
                ("w", j),
                decw_hbm.at[:, :, pl.ds(j * 128, 128)],
                w_v.at[:, :, pl.ds(cc * 1024 + q * 128, 128)],
                w_sem.at[j],
            )
        fetch("tgt", tgt_hbm.at[x], tgt_v, tgt_sem)

    fetch_layer(0)
    fetch_layer(1)

    for s in range(LAYERS):
        for t in range(s, LAYERS):
            found = jnp.int32(0)
            for k in range(10):
                hit = jnp.logical_and(pairs_ref[0, k] == s, pairs_ref[1, k] == t)
                found = jnp.where(hit, jnp.int32(k), found)
            row_s[s * 4 + t] = found

    sent = []

    def remote(source, target, send_sem, recv_sem, dev):
        return pltpu.make_async_remote_copy(
            src_ref=source, dst_ref=target, send_sem=send_sem, recv_sem=recv_sem,
            device_id=dev, device_id_type=MESH,
        )

    def gather_copy(i, kind):
        lat = lat_v.at[i]
        if kind in (A_Y, A_OWN_UP, A_OWN_DOWN):
            view = lat.at[:, block_of(place)]
        elif kind in (A_PAIR_UP, A_PAIR_DOWN):
            view = lat.at[:, block_of(z * 2 + 1 - yh)]
        elif kind == A_FWD_UP:
            view = lat.at[pl.ds(0, part), block_of(down * 2 + yh)]
        elif kind == A_FWD_DOWN:
            view = lat.at[pl.ds(part, part), block_of(up * 2 + yh)]
        elif kind == A_FAR:
            view = lat.at[:, block_of(far * 2 + yh)]
        else:
            view = lat.at[:, half_of(core)]
        if kind in (A_Y, A_FAR):
            dev = dev_y
        elif kind == A_TWIN:
            dev = dev_twin
        elif kind in (A_OWN_UP, A_PAIR_UP, A_FWD_UP):
            dev = dev_up
        else:
            dev = dev_down
        return remote(view, view, a_send.at[i, kind], a_recv.at[i, kind], dev)

    def spot(zz, hh):
        return pl.ds(at128(zz * 256 + hh * 128), 128)

    def scatter_copy(i, kind):
        other = 1 - yh
        if kind == R_TWIN:
            source, target, dev = g_v.at[i, :, half_of(1 - core)], tw_v.at[i], dev_twin
        elif kind == R_FAR:
            source, target, dev = s_v.at[i, :, spot(far, other)], fy_v.at[i], dev_y
        elif kind == R_SIDE_UP:
            source, target, dev = s_v.at[i, :, spot(up, other)], zf_v.at[i, 0, 1], dev_up
        elif kind == R_SIDE_DOWN:
            source, target, dev = s_v.at[i, :, spot(down, other)], zf_v.at[i, 1, 1], dev_down
        elif kind == R_RELAY_UP:
            source, target, dev = s_v.at[i, pl.ds(0, part), spot(far, yh)], zr_v.at[i, 0], dev_up
        elif kind == R_RELAY_DOWN:
            source, target, dev = s_v.at[i, pl.ds(part, part), spot(far, yh)], zr_v.at[i, 1], dev_down
        elif kind == R_OWN_UP:
            source, target, dev = s_v.at[i, :, spot(up, yh)], zf_v.at[i, 0, 0], dev_up
        elif kind == R_OWN_DOWN:
            source, target, dev = s_v.at[i, :, spot(down, yh)], zf_v.at[i, 1, 0], dev_down
        else:
            source, target, dev = ty_v.at[i], yr_v.at[i], dev_y
        return remote(source, target, r_send.at[i, kind], r_recv.at[i, kind], dev)

    def part_copy(h, d):
        peer = peers[d]
        source = p_snd.at[h, lax.rem(peer, 4), :, pl.ds(at128((peer // 4) * 128), 128)]
        return remote(source, p_rcv.at[h, d], p_send.at[h, d], p_recv.at[h, d], (peer, tgt))

    def error_copy(h, d):
        view = err_v.at[h, x, :, pl.ds(at128(yl * 128), 128)]
        return remote(view, view, e_send.at[h, d], e_recv.at[h, d], (peers[d], tgt))

    def start(copy):
        copy.start()
        sent.append(copy)

    def encode(h, s):
        i = h * 4 + s
        if h == 0:
            incoming[("encw", s)].wait()
            incoming[("act", s)].wait()
        have_tokens(h, s)
        if h == 0:
            if s < 2:
                fetch_layer(s + 2)
            else:
                fetch_tokens(1, 2 * (s - 2))
                fetch_tokens(1, 2 * (s - 2) + 1)
            if s == 3:
                fetch_rest()
        rows = pl.ds(h * chunk, chunk)
        pre = jnp.zeros((chunk, 128), F32)
        for n in range(blocks):
            weight = encw_v[s, n * 256 : (n + 1) * 256, :]
            pre = pre + jnp.dot(res_v[s, n, h], weight, preferred_element_type=F32)
        pre = pre + encb_ref[s : s + 1, :]
        lat_v[i, :, block_of(place)] = (pre * act_v[s, rows, :].astype(F32)).astype(BF16)
        if i == 0:
            pl.semaphore_wait(barrier, len(greeted))
        for kind in (A_OWN_UP, A_OWN_DOWN, A_Y):
            start(gather_copy(i, kind))

    def gather_pair(i):
        gather_copy(i, A_Y).wait_recv()
        start(gather_copy(i, A_PAIR_UP))
        start(gather_copy(i, A_PAIR_DOWN))

    def gather_forward(i):
        gather_copy(i, A_OWN_UP).wait_recv()
        start(gather_copy(i, A_FWD_UP))
        gather_copy(i, A_OWN_DOWN).wait_recv()
        start(gather_copy(i, A_FWD_DOWN))

    def gather_far(i):
        gather_copy(i, A_FWD_UP).wait_recv()
        gather_copy(i, A_FWD_DOWN).wait_recv()
        start(gather_copy(i, A_FAR))

    def gather_twin(i):
        gather_copy(i, A_PAIR_UP).wait_recv()
        gather_copy(i, A_PAIR_DOWN).wait_recv()
        gather_copy(i, A_FAR).wait_recv()
        start(gather_copy(i, A_TWIN))

    def recon(h, s):
        i = h * 4 + s
        gather_copy(i, A_TWIN).wait_recv()
        if i == 0:
            for j in range(16):
                incoming[("w", j)].wait()
        for t in range(s, LAYERS):
            term = lax.dot_general(
                w_v[row_s[s * 4 + t]], lat_v[i], (((1,), (1,)), ((), ())),
                preferred_element_type=F32,
            )
            if s == 0:
                p_acc[h, t] = term
            else:
                p_acc[h, t] = p_acc[h, t] + term

    def share_parts(h):
        p_snd[h] = p_acc[h].astype(BF16)
        for d in range(1, 8):
            start(part_copy(h, d))

    def make_error(h):
        own = pl.ds(at128(yl * 128), 128)
        total = p_acc[h, x, :, own]
        for d in range(1, 8):
            part_copy(h, d).wait_recv()
            total = total + p_rcv[h, d].astype(F32)
        if h == 0:
            incoming["tgt"].wait()
        bias = column_of(decb_ref[pl.ds(x, 1), :], feats)
        wanted = tgt_v[:, pl.ds(at128(h * chunk + yl * 128), 128)].astype(F32)
        err_v[h, x, :, own] = (total + bias - wanted).astype(BF16)
        for d in range(1, 8):
            start(error_copy(h, d))

    def have_error(h):
        for d in range(1, 8):
            error_copy(h, d).wait_recv()
        turn_error(h)

    def turn_error(h):
        stack = jnp.concatenate([err_v[h, t] for t in reversed(range(LAYERS))], axis=0)
        et_v[h] = stack.T

    def grad(h, s):
        i = h * 4 + s
        depth = (LAYERS - s) * feats
        step = 512

        @pl.loop(0, 2048 // step)
        def _(n):
            cols = pl.ds(pl.multiple_of(n * step, step), step)
            weights = [w_v[row_s[s * 4 + t], :, cols] for t in reversed(range(s, LAYERS))]
            stack = jnp.concatenate(weights, axis=0) if s < LAYERS - 1 else weights[0]
            g_v[i, :, cols] = jnp.dot(
                et_v[h, :, 0:depth], stack, preferred_element_type=F32
            ).astype(BF16)

        start(scatter_copy(i, R_TWIN))

    def scatter_twin(i):
        scatter_copy(i, R_TWIN).wait_recv()
        s_v[i] = (g_v[i, :, half_of(core)].astype(F32) + tw_v[i].astype(F32)).astype(BF16)
        for kind in (R_FAR, R_SIDE_UP, R_SIDE_DOWN):
            start(scatter_copy(i, kind))

    def scatter_far(i):
        scatter_copy(i, R_FAR).wait_recv()
        mine = s_v[i, :, spot(far, yh)].astype(F32)
        s_v[i, :, spot(far, yh)] = (mine + fy_v[i].astype(F32)).astype(BF16)
        start(scatter_copy(i, R_RELAY_UP))
        start(scatter_copy(i, R_RELAY_DOWN))

    def scatter_relay(i):
        for kind, rows, to, slot, last in (
            (R_RELAY_UP, pl.ds(0, part), up, 0, R_OWN_UP),
            (R_RELAY_DOWN, pl.ds(part, part), down, 1, R_OWN_DOWN),
        ):
            scatter_copy(i, kind).wait_recv()
            mine = s_v[i, rows, spot(to, yh)].astype(F32)
            s_v[i, rows, spot(to, yh)] = (mine + zr_v[i, slot].astype(F32)).astype(BF16)
            start(scatter_copy(i, last))

    def scatter_side(i):
        scatter_copy(i, R_SIDE_UP).wait_recv()
        scatter_copy(i, R_SIDE_DOWN).wait_recv()
        total = s_v[i, :, spot(z, 1 - yh)].astype(F32)
        ty_v[i] = (total + zf_v[i, 0, 1].astype(F32) + zf_v[i, 1, 1].astype(F32)).astype(BF16)
        start(scatter_copy(i, R_Y))

    def scatter_own(h, s):
        i = h * 4 + s
        scatter_copy(i, R_Y).wait_recv()
        grads = s_v[i, :, spot(z, yh)].astype(F32) + yr_v[i].astype(F32)
        scatter_copy(i, R_OWN_UP).wait_recv()
        scatter_copy(i, R_OWN_DOWN).wait_recv()
        grads = grads + zf_v[i, 0, 0].astype(F32) + zf_v[i, 1, 0].astype(F32)
        rows = pl.ds(h * chunk, chunk)
        pre = (grads * act_v[s, rows, :].astype(F32)).astype(BF16)
        pre_v[s, rows, :] = pre
        sums = jnp.sum(pre.astype(F32), axis=0, keepdims=True)
        if h == 0:
            bias_ref[s : s + 1, :] = sums
        else:
            bias_ref[s : s + 1, :] = bias_ref[s : s + 1, :] + sums

    def encoder_grad(s):
        across = pre_v[s].T

        @pl.loop(0, blocks)
        def _(n):
            block = res_v[s, n].reshape(tok, 256)
            out = jnp.dot(across, block, preferred_element_type=F32).astype(BF16)
            enc_ref[s, pl.ds(pl.multiple_of(n * 256, 256), 256), :] = out.T

    def decoder_grad(k):
        source, target = pairs_ref[0, k], pairs_ref[1, k]
        low, high = err_v[0, target], err_v[1, target]
        for cc in range(2):
            for m in range(2):
                cols = slice(cc * 1024 + m * 512, cc * 1024 + (m + 1) * 512)
                out = jnp.dot(low, lat_v[source, :, cols], preferred_element_type=F32)
                out = out + jnp.dot(high, lat_v[source + 4, :, cols], preferred_element_type=F32)
                out = out.astype(BF16)
                for j in range(4):
                    begin = ((m * 4 + j) * 2 + cc) * 128
                    dec_ref[k, :, begin : begin + 128] = out[:, j * 128 : (j + 1) * 128]

    for s in range(LAYERS):
        encode(0, s)
    gather_forward(0)
    gather_forward(1)
    gather_pair(0)
    gather_forward(2)
    gather_pair(1)
    gather_forward(3)
    gather_pair(2)
    gather_pair(3)
    for s in range(LAYERS):
        encode(1, s)
        gather_far(s)
    gather_twin(0)
    gather_forward(4)
    gather_twin(1)
    gather_forward(5)
    gather_twin(2)
    recon(0, 0)
    gather_forward(6)
    gather_pair(4)
    gather_twin(3)
    recon(0, 1)
    gather_forward(7)
    gather_pair(5)
    recon(0, 2)
    gather_pair(6)
    gather_pair(7)
    recon(0, 3)
    share_parts(0)
    gather_far(4)
    gather_far(5)
    gather_far(6)
    gather_twin(4)
    make_error(0)
    gather_far(7)
    gather_twin(5)
    recon(1, 0)
    gather_twin(6)
    recon(1, 1)
    have_error(0)
    grad(0, 3)
    gather_twin(7)
    grad(0, 2)
    recon(1, 2)
    scatter_twin(3)
    recon(1, 3)
    share_parts(1)
    scatter_twin(2)
    grad(0, 1)
    scatter_far(3)
    grad(0, 0)
    scatter_twin(1)
    scatter_side(3)
    make_error(1)
    scatter_far(2)
    scatter_twin(0)
    scatter_side(2)
    scatter_relay(3)
    scatter_far(1)
    scatter_side(1)
    scatter_relay(2)
    have_error(1)
    grad(1, 3)
    grad(1, 2)
    scatter_twin(7)
    scatter_own(0, 3)
    scatter_far(0)
    scatter_side(0)
    scatter_relay(1)
    grad(1, 1)
    scatter_twin(6)
    scatter_own(0, 2)
    scatter_relay(0)
    scatter_far(7)
    grad(1, 0)
    scatter_twin(5)
    scatter_side(7)
    scatter_own(0, 1)
    scatter_own(0, 0)
    scatter_far(6)
    scatter_twin(4)
    scatter_side(6)
    decoder_grad(0)
    decoder_grad(1)
    scatter_relay(7)
    scatter_far(5)
    scatter_side(5)
    decoder_grad(2)
    decoder_grad(3)
    scatter_relay(6)
    scatter_far(4)
    scatter_side(4)
    decoder_grad(4)
    decoder_grad(5)
    scatter_own(1, 3)
    scatter_relay(5)
    encoder_grad(3)
    decoder_grad(6)
    scatter_relay(4)
    scatter_own(1, 2)
    encoder_grad(2)
    decoder_grad(7)
    decoder_grad(8)
    scatter_own(1, 1)
    encoder_grad(1)
    decoder_grad(9)
    scatter_own(1, 0)
    encoder_grad(0)
    for copy in sent:
        copy.wait_send()


def deliver(dec_ref, enc_ref, bias_ref, dec_out, enc_out, bias_out, sem):
    copies = [
        pltpu.make_async_copy(one, out, sem.at[n])
        for n, (one, out) in enumerate(((dec_ref, dec_out), (enc_ref, enc_out), (bias_ref, bias_out)))
    ]
    for copy in copies:
        copy.start()
    for copy in copies:
        copy.wait()


def shards(residual, targets, enc_weight, enc_bias, active, dec_weight, dec_bias, tile_pairs):
    layers, tok, width = residual.shape
    feats = targets.shape[1]
    own = enc_weight.shape[2]
    rows, _, block = dec_weight.shape
    chunk = tok // HALVES
    any_space = pl.BlockSpec(memory_space=pl.ANY)
    vmem = pl.BlockSpec(memory_space=pltpu.VMEM)
    dma = pltpu.SemaphoreType.DMA
    blocks = width // 256
    held = pl.pallas_call(
        kernel,
        out_shape=(
            pltpu.VMEM((rows, feats, block), BF16),
            pltpu.VMEM((layers, width, own), BF16),
            pltpu.VMEM((layers, own), F32),
        ),
        in_specs=[
            any_space, any_space, any_space, vmem, any_space, any_space, vmem,
            pl.BlockSpec(memory_space=pltpu.SMEM),
        ],
        out_specs=(vmem, vmem, vmem),
        scratch_shapes=[
            pltpu.VMEM((layers, blocks, HALVES, chunk, 256), BF16),
            pltpu.VMEM((feats, tok), BF16),
            pltpu.VMEM((layers, width, own), BF16),
            pltpu.VMEM((layers, tok, own), jnp.int32),
            pltpu.VMEM((rows, feats, block), BF16),
            pltpu.VMEM((ITEMS, chunk, block), BF16),
            pltpu.VMEM((HALVES, layers, feats, chunk), F32),
            pltpu.VMEM((HALVES, layers, feats, chunk), BF16),
            pltpu.VMEM((HALVES, 8, feats, 128), BF16),
            pltpu.VMEM((HALVES, layers, feats, chunk), BF16),
            pltpu.VMEM((ITEMS, chunk, block), BF16),
            pltpu.VMEM((ITEMS, chunk, block // 2), BF16),
            pltpu.VMEM((ITEMS, chunk, block // 2), BF16),
            pltpu.VMEM((ITEMS, chunk, own), BF16),
            pltpu.VMEM((ITEMS, 2, chunk // 2, own), BF16),
            pltpu.VMEM((ITEMS, 2, 2, chunk, own), BF16),
            pltpu.VMEM((ITEMS, chunk, own), BF16),
            pltpu.VMEM((ITEMS, chunk, own), BF16),
            pltpu.VMEM((layers, tok, own), BF16),
            pltpu.VMEM((HALVES, chunk, layers * feats), BF16),
            pltpu.SMEM((16,), jnp.int32),
            dma((layers, HALVES)), dma((layers,)), dma((layers,)), dma((16,)), dma,
            dma((ITEMS, 9)), dma((ITEMS, 9)), dma((ITEMS, 9)), dma((ITEMS, 9)),
            dma((HALVES, 8)), dma((HALVES, 8)), dma((HALVES, 8)), dma((HALVES, 8)),
        ],
        compiler_params=pltpu.CompilerParams(
            collective_id=0, has_side_effects=True, vmem_limit_bytes=58000000
        ),
    )(residual, targets, enc_weight, enc_bias, active, dec_weight, dec_bias, tile_pairs.T)
    return pl.pallas_call(
        deliver,
        out_shape=tuple(jax.ShapeDtypeStruct(one.shape, one.dtype) for one in held),
        in_specs=[any_space] * 3,
        out_specs=(any_space,) * 3,
        scratch_shapes=[dma((3,))],
        compiler_params=pltpu.CompilerParams(vmem_limit_bytes=1 << 20),
    )(*held)


def solution(mesh):
    in_specs = (
        P(),
        P(None, "tgt", None),
        P(None, None, ("src", "tgt")),
        P(None, ("src", "tgt")),
        P(None, None, ("src", "tgt")),
        P("src", "tgt", None),
        P(None, "tgt"),
        P("src", None),
    )
    out_specs = (P("src", "tgt", None), P(None, None, ("src", "tgt")), P(None, ("src", "tgt")))
    return jax.shard_map(shards, mesh=mesh, in_specs=in_specs, out_specs=out_specs, check_vma=False)
```

time: 120 us -> 103 us (0.86)
  local copies, waits for them, and re-layouts: 9.77 us -> 0 us
  Pallas kernels: 109 us -> 102 us
    unnamed x8 -> x0, local copies, waits for them, and re-layouts: 9.77 us -> none
    pallas_call x1 -> x2, Pallas kernels: 109 us -> 102 us  [the longest x1 98.6 us: shards(): pl.pallas_call(kernel, out_shape=(pltpu.VMEM((rows, feats, block), BF16),...]
where the time goes in v2:
time: 103 us
  Pallas kernels  102 us (99%)
    pallas_call x1, Pallas kernels, shards(): pl.pallas_call(kernel, out_shape=(pltpu.VMEM((rows, feats, block), BF16),...  98.6 us
    pallas_call x1, Pallas kernels, shards(): pl.pallas_call(deliver, out_shape=tuple((jax.ShapeDtypeStruct(one.shape,...  3.38 us

profile of v2, /device:TPU:0, one launch (start us, length us, event | category | flops | bytes accessed | tf_op | source)
XLA Modules:
  0.0 102.8 jit_solution(11142822132650849833)
XLA Ops:
  0.6 98.6 %shard_map.103 = (bf16[10,144,2048]{2,1,0:T(8,128)(2,1)S(1)}, bf16[4,2304,128]{2,1,0:T(8,128)(2,1)S(1)}, f32[4,128]{1,0:T(4,128)S(1)}) custom-call(bf16[4,512,2304]{2,1,0:T(8,128)(2,1)} %res_hbm.1, bf16[4,144,512]{2,1,0:T(8,128)(2,1)} %tgt_hbm.1, bf16[4,2304,128]{2,1,0:T(8,128)(2,1)} %encw_hbm.1, f32[4,128]{1,0:T(4,128)} %encb_ref.1, ...), custom_call_target="tpu_custom_call" | custom-call | tf_op jit(solution)/shard_map/pallas_call | solution.py:495
  99.3 3.4 %shard_map.104 = (bf16[10,144,2048]{2,1,0:T(8,128)(2,1)}, bf16[4,2304,128]{2,1,0:T(8,128)(2,1)}, f32[4,128]{1,0:T(4,128)}) custom-call(bf16[10,144,2048]{2,1,0:T(8,128)(2,1)S(1)} %get-tuple-element.6.dec_ref, bf16[4,2304,128]{2,1,0:T(8,128)(2,1)S(1)} %get-tuple-element.7.enc_ref, f32[4,128]{1,0:T(4,128)S(1)} %get-tuple-element.8.bias_ref), custom_call_target="tpu_custom_call" | custom-call | tf_op jit(solution)/shard_map/pallas_call | solution.py:537

commit v3 on v2

--- a/solution.py
+++ b/solution.py
@@ -205,8 +205,13 @@
         lat_v[i, :, block_of(place)] = (pre * act_v[s, rows, :].astype(F32)).astype(BF16)
         if i == 0:
             pl.semaphore_wait(barrier, len(greeted))
-        for kind in (A_OWN_UP, A_OWN_DOWN, A_Y):
-            start(gather_copy(i, kind))
+        start(gather_copy(i, A_Y))
+        if h == 0:
+            send_own(i)
+
+    def send_own(i):
+        start(gather_copy(i, A_OWN_UP))
+        start(gather_copy(i, A_OWN_DOWN))
 
     def gather_pair(i):
         gather_copy(i, A_Y).wait_recv()
@@ -279,7 +284,7 @@
         depth = (LAYERS - s) * feats
         step = 512
 
-        @pl.loop(0, 2048 // step)
+        @pl.loop(0, 2048 // step, unroll=4)
         def _(n):
             cols = pl.ds(pl.multiple_of(n * step, step), step)
             weights = [w_v[row_s[s * 4 + t], :, cols] for t in reversed(range(s, LAYERS))]
@@ -339,7 +344,7 @@
     def encoder_grad(s):
         across = pre_v[s].T
 
-        @pl.loop(0, blocks)
+        @pl.loop(0, blocks, unroll=9)
         def _(n):
             block = res_v[s, n].reshape(tok, 256)
             out = jnp.dot(across, block, preferred_element_type=F32).astype(BF16)
@@ -361,15 +366,20 @@
     for s in range(LAYERS):
         encode(0, s)
     gather_forward(0)
+    encode(1, 0)
     gather_forward(1)
     gather_pair(0)
+    encode(1, 1)
     gather_forward(2)
     gather_pair(1)
+    encode(1, 2)
     gather_forward(3)
     gather_pair(2)
+    encode(1, 3)
     gather_pair(3)
     for s in range(LAYERS):
-        encode(1, s)
+        send_own(4 + s)
+    for s in range(LAYERS):
         gather_far(s)
     gather_twin(0)
     gather_forward(4)

time: 103 us -> 94.7 us (0.919)
  Pallas kernels: 102 us -> 93.1 us
    pallas_call x1, Pallas kernels: 98.6 us -> 89.8 us  [shards(): pl.pallas_call(kernel, out_shape=(pltpu.VMEM((rows, feats, block), BF16),...]
where the time goes in v3:
time: 94.7 us; the launch traced here: 93.9 us
  Pallas kernels  93.1 us (98%)
    pallas_call x1, Pallas kernels, shards(): pl.pallas_call(kernel, out_shape=(pltpu.VMEM((rows, feats, block), BF16),...  89.8 us
    pallas_call x1, Pallas kernels, shards(): pl.pallas_call(deliver, out_shape=tuple((jax.ShapeDtypeStruct(one.shape,...  3.38 us

profile of v3, /device:TPU:0, one launch (start us, length us, event | category | flops | bytes accessed | tf_op | source)
XLA Modules:
  0.0 93.9 jit_solution(919803575230621383)
XLA Ops:
  0.6 89.8 %shard_map.103 = (bf16[10,144,2048]{2,1,0:T(8,128)(2,1)S(1)}, bf16[4,2304,128]{2,1,0:T(8,128)(2,1)S(1)}, f32[4,128]{1,0:T(4,128)S(1)}) custom-call(bf16[4,512,2304]{2,1,0:T(8,128)(2,1)} %res_hbm.1, bf16[4,144,512]{2,1,0:T(8,128)(2,1)} %tgt_hbm.1, bf16[4,2304,128]{2,1,0:T(8,128)(2,1)} %encw_hbm.1, f32[4,128]{1,0:T(4,128)} %encb_ref.1, ...), custom_call_target="tpu_custom_call" | custom-call | tf_op jit(solution)/shard_map/pallas_call | solution.py:505
  90.4 3.4 %shard_map.104 = (bf16[10,144,2048]{2,1,0:T(8,128)(2,1)}, bf16[4,2304,128]{2,1,0:T(8,128)(2,1)}, f32[4,128]{1,0:T(4,128)}) custom-call(bf16[10,144,2048]{2,1,0:T(8,128)(2,1)S(1)} %get-tuple-element.6.dec_ref, bf16[4,2304,128]{2,1,0:T(8,128)(2,1)S(1)} %get-tuple-element.7.enc_ref, f32[4,128]{1,0:T(4,128)S(1)} %get-tuple-element.8.bias_ref), custom_call_target="tpu_custom_call" | custom-call | tf_op jit(solution)/shard_map/pallas_call | solution.py:547
